TPU v7x, 32 devices: a whole 2x2x4 slice. The times are simulated.
32 devices in a mesh: dp: 16 (over z, y, x), section: 2 (over core).
Axes of the slice: x: 2, y: 2, z: 4, core: 2. Of those that a mesh axis runs over, the one named last changes fastest.
Arguments:
- acts: bfloat16 [2, 2, 2048, 2048], P('section', None, 'dp'), may hold values from -6 to 6
- cotan: bfloat16 [2, 2, 2048, 384], P('section', None, 'dp'), may hold values from -0.09375 to 0.09375
- counts: int32 [2, 2, 16, 1], P('section', None, 'dp'), may hold values from 32 to 128
- weight: float32 [2, 786432], P('section', 'dp'), may hold values from -4 to 4
- moment: float32 [2, 786432], P('section', 'dp'), may hold values from -4 to 4
- second: float32 [2, 786432], P('section', 'dp'), may hold values from 0.1 to 1
Outputs:
- new_weight: float32 [2, 786432], P('section', 'dp')
- new_moment: float32 [2, 786432], P('section', 'dp')
- new_second: float32 [2, 786432], P('section', 'dp')
All inputs are finite; a program needn't handle non-finite values.
Results may differ from a plain program's by a relative error of at most 0.0003.
Values sent between devices are 32-bit elements; how exact they have to be, the bound alone decides.
A program may use at most 64 MiB of HBM per device.

v0:
```python
import jax
import jax.numpy as jnp
from jax import lax
from jax.sharding import PartitionSpec as P


def swapped(array, axis, stride):
    return lax.ppermute(array, axis, [(i, i ^ 1 << stride) for i in range(lax.axis_size(axis))])


def adamw_shard(grad, weight_now, moment_now, second_now):
    new_m = 0.9 * moment_now + 0.1 * grad
    new_v = 0.95 * second_now + 0.05 * grad * grad
    corr_m = new_m / (1.0 - 0.9**10)
    corr_v = new_v / (1.0 - 0.95**10)
    new_w = weight_now - 0.01 * (corr_m / (jnp.sqrt(corr_v) + 1e-08) + 0.1 * weight_now)
    return (new_w, new_m, new_v)


def shards(acts, cotan, counts, weight, moment, second):
    micro = counts.shape[3]
    rows = acts.shape[2]
    slots = rows // micro
    place = lax.broadcasted_iota(jnp.int32, (micro, slots), 1)
    live = (place[None] < counts[0, :, 0, :, None]).reshape(2, rows)
    masked = cotan[0] * live.astype(jnp.bfloat16)[:, :, None]
    grads = jnp.einsum("krd,krf->kdf", acts[0], masked, preferred_element_type=jnp.float32)
    own_grad = grads[0].reshape(-1)
    far_grad = grads[1].reshape(-1)
    section_bits = lax.axis_size("section").bit_length() - 1
    for bit in range(section_bits):
        far_grad = swapped(far_grad, "section", bit)
    shard = lax.psum_scatter(own_grad + far_grad, "dp", scatter_dimension=0, tiled=True)
    new_w, new_m, new_v = adamw_shard(shard, weight[0], moment[0], second[0])
    return (new_w[None], new_m[None], new_v[None])


def solution(mesh):
    in_specs = (
        P("section", None, "dp", None),
        P("section", None, "dp", None),
        P("section", None, "dp", None),
        P("section", "dp"),
        P("section", "dp"),
        P("section", "dp"),
    )
    out_specs = (P("section", "dp"), P("section", "dp"), P("section", "dp"))
    return jax.shard_map(shards, mesh=mesh, in_specs=in_specs, out_specs=out_specs, check_vma=False)
```

profile of v0, /device:TPU:0, one launch (start us, length us, event | category | flops | bytes accessed | tf_op | source)
XLA Modules:
  0.0 193.1 jit_solution(1944388499101270658)
XLA Ops:
  7.2 0.0 copy-start
  7.2 0.0 all-reduce.3.cloned.1.call-start
  7.2 0.8 compare_convert_fusion
  8.0 0.4 copy-done
  8.4 2.0 %convolution_bitcast_fusion = f32[2,2048,384]{1,2,0:T(8,128)S(1)} fusion(bf16[1,2,128,2048]{3,2,1,0:T(8,128)(2,1)S(1)} %copy-done, bf16[1,2,128,384]{3,2,1,0:T(8,128)(2,1)} %param.7, bf16[2,128]{1,0:T(2,128)(2,1)S(1)} %compare_convert_fusion), kind=kOutput, calls=%fused_computation | convolution fusion | flops 402751488 | bytes 7537152 | tf_op jit(solution)/shard_map/krd,krf->kdf/dot_general | solution.py:27
  10.4 3.1 %fusion.4 = (f32[1,2048,384]{1,2,0:T(8,128)}, f32[1,2048,384]{1,2,0:T(8,128)}) fusion(f32[2,2048,384]{1,2,0:T(8,128)S(1)} %convolution_bitcast_fusion), kind=kLoop, calls=%fused_computation.11 | loop fusion | bytes 12582912 | tf_op jit(solution)/shard_map/slice | solution.py:29
  13.5 3.5 %copy.15 = f32[1,2048,384]{2,1,0:T(8,128)} copy(f32[1,2048,384]{1,2,0:T(8,128)} %get-tuple-element.6) | data formatting | bytes 6291456 | tf_op jit(solution)/shard_map/slice | solution.py:29
  17.1 0.0 copy-start.2
  17.1 4.5 %reshape_squeeze.7 = f32[786432]{0:T(1024)} reshape(f32[1,2048,384]{2,1,0:T(8,128)} %copy.15) | data formatting | bytes 6291456 | tf_op jit(solution)/shard_map/reshape;squeeze | solution.py:29
  21.6 0.5 collective-permute-start
  22.1 0.0 copy-done.2
  22.1 0.2 broadcast_multiply_fusion.1
  22.3 3.5 %copy.14 = f32[1,2048,384]{2,1,0:T(8,128)} copy(f32[1,2048,384]{1,2,0:T(8,128)} %get-tuple-element.7) | data formatting | bytes 6291456 | tf_op jit(solution)/shard_map/slice | solution.py:28
  25.8 4.4 %reshape_squeeze.6 = f32[786432]{0:T(1024)} reshape(f32[1,2048,384]{2,1,0:T(8,128)} %copy.14) | data formatting | bytes 6291456 | tf_op jit(solution)/shard_map/reshape;squeeze | solution.py:28
  30.2 0.0 collective-permute-done
  30.2 4.9 %add.20 = f32[786432]{0:T(1024)} add(f32[786432]{0:T(1024)} %reshape_squeeze.6, f32[786432]{0:T(1024)} %collective-permute-done) | non-fusion elementwise | flops 786432 | bytes 9437184 | tf_op jit(solution)/shard_map/add | solution.py:33
  35.1 0.0 all-reduce.3.cloned.1.call-update
  35.1 0.9 copy-done.3
  36.0 0.2 broadcast_multiply_fusion
  36.2 0.0 copy-done.4
  36.2 0.6 dynamic-slice
  37.5 147.0 %all-reduce.3.cloned.1.call-done = f32[786432]{0:T(1024)} async-done(((f32[786432]{0:T(1024)}), f32[786432]{0:T(1024)}) %all-reduce.3.cloned.1.call-update) | async-done | bytes 3145744
  184.5 0.0 copy-done.1
  184.5 1.8 multiply_subtract_fusion
  (3 shorter events, 0.0 us)
Async XLA Ops:
  7.2 1.2 copy-start
  7.2 177.3 %all-reduce.3.cloned.1.call-start = ((), (), s32[]{:S(2)}) async-start(), calls=%async_computation | async-start | bytes 6291456
  17.1 5.0 %copy-start.2 = (f32[1,49152]{1,0:T(1,128)S(1)}, f32[1,49152]{1,0:T(1,128)}, u32[]{:S(2)}) copy-start(f32[1,49152]{1,0:T(1,128)} %param.10) | copy-start | bytes 589828
  21.6 8.7 %collective-permute-start = (f32[786432]{0:T(1024)}, f32[786432]{0:T(1024)}, u32[]{:S(2)}, u32[]{:S(2)}) collective-permute-start(f32[786432]{0:T(1024)} %reshape_squeeze.7), channel_id=1, source_target_pairs={{0,1},{1,0},{2,3},{3,2},{4,5},{5,4},{6,7},{7,6},{8,9},{9,8},{10,11... | collective-permute-start | bytes 9437192 | tf_op jit(solution)/shard_map/ppermute | solution.py:8
  35.1 0.9 copy-start.3
  35.1 1.1 copy-start.4
  35.1 149.4 %copy-start.1 = (f32[1,49152]{1,0:T(1,128)S(1)}, f32[1,49152]{1,0:T(1,128)}, u32[]{:S(2)}) copy-start(f32[1,49152]{1,0:T(1,128)} %param.9) | copy-start | bytes 589828
Sparse Core Ops, SparseCore 0:
  35.2 149.1 all-reduce.2
where the time goes:
time: 194 us; the launch traced here: 193 us
  waiting for transfers between devices  147 us (76%)
  local copies, waits for them, and re-layouts  21 us (11%)
  between operations  14.7 us (8%)
  other arithmetic  7.87 us (4%)
  matrix products  2.01 us (1%)
    unnamed x2, waiting for transfers between devices  147 us
    slice x2, local copies, waits for them, and re-layouts, shards(): far_grad = grads[1].reshape(-1)  6.63 us
    add x1, other arithmetic, shards(): own_grad + far_grad  4.85 us
    another operation x1, local copies, waits for them, and re-layouts, shards(): far_grad = grads[1].reshape(-1)  4.52 us
    another operation x1, local copies, waits for them, and re-layouts, shards(): own_grad = grads[0].reshape(-1)  4.43 us
  transfers between devices with their start and end apart: 2, of which 1 were waited for; matrix products, arithmetic and copies ran while one was open for 5% of the time, Pallas kernels for 0%

commit v1 on v0

v1 whole, which is shorter than its diff:
```python
import functools
import jax
import jax.numpy as jnp
from jax import lax
from jax.experimental import pallas as pl
from jax.experimental.pallas import tpu as pltpu
from jax.sharding import PartitionSpec as P

LANES = 128
MESH = pl.DeviceIdType.MESH


def adamw_shard(grad, weight_now, moment_now, second_now):
    new_m = 0.9 * moment_now + 0.1 * grad
    new_v = 0.95 * second_now + 0.05 * grad * grad
    corr_m = new_m / (1.0 - 0.9**10)
    corr_v = new_v / (1.0 - 0.95**10)
    new_w = weight_now - 0.01 * (corr_m / (jnp.sqrt(corr_v) + 1e-08) + 0.1 * weight_now)
    return (new_w, new_m, new_v)


def dp_digits(mesh):
    size = mesh.shape["dp"]
    line = mesh.devices.reshape(size, -1)[:, 0]
    digits = []
    if hasattr(line[0], "coords"):
        for axis in range(3):
            at = [device.coords[axis] for device in line]
            if len(set(at)) > 1:
                digits.append((len(set(at)), next(j for j in range(size) if at[j] != at[0])))
    total = 1
    for count, stride in digits:
        total *= count
    if total != size:
        digits = [(size, 1)] if size > 1 else []
    digits.sort()
    return [(1, 1)] * (3 - len(digits)) + digits


def reduce_kernel(digits, micro, acts, cotan, counts, out, acts_out, cotan_out, acts_in, cotan_in, lhs, rhs, grad, got1, got2, got3,
                  part_send, part_recv, send1, recv1, send2, recv2, send3, recv3):
    sections = lax.axis_size("section")
    section = lax.axis_index("section")
    dp = lax.axis_index("dp")
    mirror = sections - 1 - section
    (count_a, stride_a), (count_b, stride_b), (count_c, stride_c) = digits

    def moved(step, digit):
        count, stride = digit
        mine = lax.rem(lax.div(dp, stride), count)
        return (lax.rem(mine + step, count) - mine) * stride

    peers = [(dp, mirror)]
    for digit in digits:
        peers += [(dp + moved(step, digit), section) for step in range(1, digit[0])]
    barrier = pltpu.get_barrier_semaphore()
    for peer in peers:
        pl.semaphore_signal(barrier, inc=1, device_id=peer, device_id_type=MESH)

    rows, depth = acts.shape[1], acts.shape[2]
    width = cotan.shape[2]
    slots = rows // micro

    def masked(k):
        pieces = []
        for b in range(micro):
            block = cotan[k, b * slots:(b + 1) * slots, :].astype(jnp.float32)
            place = lax.broadcasted_iota(jnp.int32, (slots, width), 0)
            pieces.append(jnp.where(place < counts[k, b], block, 0.0))
        return pieces[0] if micro == 1 else jnp.concatenate(pieces, axis=0)

    cotan_out[...] = masked(1)
    acts_out[...] = acts[1].astype(jnp.float32)
    pl.semaphore_wait(barrier, len(peers))

    def to_mirror(src, dst, at):
        return pltpu.make_async_remote_copy(
            src_ref=src, dst_ref=dst, send_sem=part_send.at[at], recv_sem=part_recv.at[at],
            device_id=(dp, mirror), device_id_type=MESH)

    exchange = [to_mirror(cotan_out, cotan_in, 0), to_mirror(acts_out, acts_in, 1)]
    for copy in exchange:
        copy.start()
    lhs[0:rows, :] = acts[0]
    rhs[0:rows, :] = masked(0).astype(jnp.bfloat16)
    for copy in exchange:
        copy.wait_recv()
    rhs[rows:2 * rows, :] = cotan_in[...].astype(jnp.bfloat16)
    lhs[rows:2 * rows, :] = acts_in[...].astype(jnp.bfloat16)

    per_row = width // LANES
    tile = 256
    for t in range(depth // tile):
        product = lax.dot_general(
            lhs[:, t * tile:(t + 1) * tile], rhs[...], (((0,), (0,)), ((), ())), preferred_element_type=jnp.float32)
        for c in range(per_row):
            grad[pl.ds(t * tile * per_row + c, tile, stride=per_row), :] = product[:, c * LANES:(c + 1) * LANES]

    shard_rows = out.shape[0]
    half = shard_rows // 2
    orders = ((digits[0], digits[1]), (digits[1], digits[0]))
    last = digits[2]

    def block(o, step1, step2, step3):
        first, second = orders[o]
        owner = dp + moved(step1, first) + moved(step2, second) + moved(step3, last)
        return grad.at[pl.ds(pl.multiple_of(owner * shard_rows + o * half, 8), half), :]

    def base1(o, step1, step2, step3):
        first, second = orders[o]
        return ((step1 - 1) * second[0] + step2) * last[0] + step3

    def stage1(o, step1, step2, step3):
        at = base1(o, step1, step2, step3)
        return pltpu.make_async_remote_copy(
            src_ref=block(o, step1, step2, step3), dst_ref=got1[o].at[at], send_sem=send1[o].at[at], recv_sem=recv1[o].at[at],
            device_id=(dp + moved(step1, orders[o][0]), section), device_id_type=MESH)

    def stage2(o, step2, step3):
        at = (step2 - 1) * last[0] + step3
        return pltpu.make_async_remote_copy(
            src_ref=block(o, 0, step2, step3), dst_ref=got2[o].at[at], send_sem=send2[o].at[at], recv_sem=recv2[o].at[at],
            device_id=(dp + moved(step2, orders[o][1]), section), device_id_type=MESH)

    def stage3(o, step3):
        at = step3 - 1
        return pltpu.make_async_remote_copy(
            src_ref=block(o, 0, 0, step3), dst_ref=got3[o].at[at], send_sem=send3[o].at[at], recv_sem=recv3[o].at[at],
            device_id=(dp + moved(step3, last), section), device_id_type=MESH)

    started = []

    def start(copy):
        copy.start()
        started.append(copy)

    def arrived1(o, step2, step3):
        total = block(o, 0, step2, step3)[...]
        for step1 in range(1, orders[o][0][0]):
            stage1(o, step1, step2, step3).wait_recv()
            total += got1[o][base1(o, step1, step2, step3)]
        return total

    def arrived2(o, step3):
        total = arrived1(o, 0, step3)
        for step2 in range(1, orders[o][1][0]):
            stage2(o, step2, step3).wait_recv()
            total += got2[o][(step2 - 1) * last[0] + step3]
        return total

    steps3 = sorted(range(1, last[0]), key=lambda step: -min(step, last[0] - step)) + [0]

    def send_forward(i):
        if i < len(steps3):
            for o in range(2):
                for step1 in range(1, orders[o][0][0]):
                    for step2 in range(1, orders[o][1][0]):
                        start(stage1(o, step1, step2, steps3[i]))

    def send_own(i):
        if i < len(steps3):
            for o in range(2):
                for step1 in range(1, orders[o][0][0]):
                    start(stage1(o, step1, 0, steps3[i]))

    def send_second(i):
        for o in range(2):
            for step2 in range(1, orders[o][1][0]):
                block(o, 0, step2, steps3[i])[...] = arrived1(o, step2, steps3[i])
                start(stage2(o, step2, steps3[i]))

    def send_third(i):
        for o in range(2):
            block(o, 0, 0, steps3[i])[...] = arrived2(o, steps3[i])
            start(stage3(o, steps3[i]))

    send_forward(0)
    send_own(0)
    send_forward(1)
    for i in range(len(steps3)):
        send_second(i)
        send_own(i + 1)
        send_forward(i + 2)
        if i >= 1:
            send_third(i - 1)
    for o in range(2):
        total = arrived2(o, 0)
        for step3 in range(1, last[0]):
            stage3(o, step3).wait_recv()
            total += got3[o][step3 - 1]
        out[o * half:(o + 1) * half, :] = total
    for copy in exchange + started:
        copy.wait_send()


def shards(digits, acts, cotan, counts, weight, moment, second):
    micro = counts.shape[3]
    rows, depth = acts.shape[2], acts.shape[3]
    width = cotan.shape[3]
    shard_rows = weight.shape[1] // LANES
    half = shard_rows // 2
    counts1 = [(first - 1) * other * digits[2][0] for first, other in ((digits[0][0], digits[1][0]), (digits[1][0], digits[0][0]))]
    counts2 = [(other - 1) * digits[2][0] for other in (digits[1][0], digits[0][0])]
    counts3 = [digits[2][0] - 1] * 2

    def buffers(sizes):
        return [pltpu.VMEM((max(size, 1), half, LANES), jnp.float32) for size in sizes]

    def semaphores(sizes):
        return [pltpu.SemaphoreType.DMA((max(size, 1),)) for size in sizes]

    vmem = pl.BlockSpec(memory_space=pltpu.VMEM)
    shard = pl.pallas_call(
        functools.partial(reduce_kernel, digits, micro),
        out_shape=jax.ShapeDtypeStruct((shard_rows, LANES), jnp.float32),
        in_specs=[vmem, vmem, pl.BlockSpec(memory_space=pltpu.SMEM)],
        out_specs=vmem,
        scratch_shapes=[
            pltpu.VMEM((rows, depth), jnp.float32),
            pltpu.VMEM((rows, width), jnp.float32),
            pltpu.VMEM((rows, depth), jnp.float32),
            pltpu.VMEM((rows, width), jnp.float32),
            pltpu.VMEM((2 * rows, depth), jnp.bfloat16),
            pltpu.VMEM((2 * rows, width), jnp.bfloat16),
            pltpu.VMEM((depth * width // LANES, LANES), jnp.float32),
            buffers(counts1), buffers(counts2), buffers(counts3),
            pltpu.SemaphoreType.DMA((2,)), pltpu.SemaphoreType.DMA((2,)),
            semaphores(counts1), semaphores(counts1), semaphores(counts2), semaphores(counts2),
            semaphores(counts3), semaphores(counts3),
        ],
        compiler_params=pltpu.CompilerParams(collective_id=0, has_side_effects=True),
        name="reduce_grad",
    )(acts[0], cotan[0], counts[0, :, 0, :])
    new_w, new_m, new_v = adamw_shard(shard.reshape(1, -1), weight, moment, second)
    return (new_w, new_m, new_v)


def solution(mesh):
    in_specs = (
        P("section", None, "dp", None),
        P("section", None, "dp", None),
        P("section", None, "dp", None),
        P("section", "dp"),
        P("section", "dp"),
        P("section", "dp"),
    )
    out_specs = (P("section", "dp"), P("section", "dp"), P("section", "dp"))
    body = functools.partial(shards, dp_digits(mesh))
    return jax.shard_map(body, mesh=mesh, in_specs=in_specs, out_specs=out_specs, check_vma=False)
```

time: 194 us -> 45.8 us (0.24)
  waiting for transfers between devices: 147 us -> 0 us
  Pallas kernels: 0 us -> 40.6 us
  local copies, waits for them, and re-layouts: 21 us -> 1.31 us
  between operations: 14.7 us -> 0.67 us
  other arithmetic: 7.87 us -> 3.07 us
  matrix products: 2.01 us -> 0 us
    unnamed x2 -> x0, waiting for transfers between devices: 147 us -> none
    pallas_call x0 -> x1, Pallas kernels: none -> 40.6 us  [shards(): pl.pallas_call(functools.partial(reduce_kernel, digits, micro), out_shape...]
    slice x3 -> x0, local copies, waits for them, and re-layouts: 10.2 us -> none  [the longest x2 6.63 us: shards(): far_grad = grads[1].reshape(-1)]
    another operation x2 -> x0, local copies, waits for them, and re-layouts: 8.94 us -> none  [the longest x1 4.52 us: shards(): far_grad = grads[1].reshape(-1)]
    add x1 -> x0, other arithmetic: 4.85 us -> none  [shards(): own_grad + far_grad]
    dot_general x1 -> x0, matrix products: 2.01 us -> none  [shards(): jnp.einsum('krd,krf->kdf', acts[0], masked, preferred_element_type=jnp.fl...]
  transfers between devices with their start and end apart: 2 -> 0, of which waited for: 1 -> 0; matrix products, arithmetic and copies ran while one was open for 5% -> 0% of each run, Pallas kernels for 0% -> 0%
where the time goes in v1:
time: 45.8 us; the launch traced here: 45.7 us
  Pallas kernels  40.6 us (89%)
  other arithmetic  3.07 us (7%)
  local copies, waits for them, and re-layouts  1.31 us (3%)
  between operations  0.67 us (1%)
    pallas_call x1, Pallas kernels, shards(): pl.pallas_call(functools.partial(reduce_kernel, digits, micro), out_shape...  40.6 us
    sub x1, other arithmetic, adamw_shard(): weight_now - 0.01 * (corr_m / (jnp.sqrt(corr_v) + 1e-08) + 0.1 * weight_now)  3.07 us

profile of v1, /device:TPU:0, one launch (start us, length us, event | category | flops | bytes accessed | tf_op | source)
XLA Modules:
  0.0 45.7 jit_solution(6486932845317349547)
XLA Ops:
  0.6 0.0 copy-start.3
  0.6 0.6 %copy-done.3 = s32[1,2,1,1]{1,3,2,0:T(1,128)S(1)} copy-done((s32[1,2,1,1]{1,3,2,0:T(1,128)S(1)}, s32[1,2,1,1]{1,3,2,0:T(1,128)}, u32[]{:S(2)}) %copy-start.3) | copy-done | bytes 32
  1.3 0.6 %copy.9.counts = s32[2,1]{1,0:T(2,128)} copy(s32[2,1]{0,1:T(1,128)S(1)} %bitcast.7) | data formatting | bytes 16 | tf_op jit(solution)/shard_map/squeeze | solution.py:233
  1.9 0.0 copy-start
  1.9 0.0 copy-start.1
  1.9 0.0 copy-start.2
  1.9 40.6 %reduce_grad.1 = f32[384,128]{1,0:T(8,128)} custom-call(bf16[2,128,2048]{2,1,0:T(8,128)(2,1)} %bitcast.4, bf16[2,128,384]{2,1,0:T(8,128)(2,1)} %bitcast.6, s32[2,1]{1,0:T(2,128)} %copy.9.counts), custom_call_target="tpu_custom_call" | custom-call | tf_op jit(solution)/shard_map/reduce_grad/pallas_call | solution.py:213
  42.6 0.0 copy-done
  42.6 0.0 copy-done.1
  42.6 0.0 copy-done.2
  42.6 3.1 %multiply_subtract_fusion = (f32[1,49152]{1,0:T(1,128)}, f32[1,49152]{1,0:T(1,128)}, f32[1,49152]{1,0:T(1,128)}) fusion(f32[1,49152]{1,0:T(1,128)S(1)} %copy-done, f32[1,49152]{1,0:T(1,128)} %bitcast.5, f32[1,49152]{1,0:T(1,128)S(1)} %copy-done.1, f32[1,49152]{1,0:T(1,128)S(1)} %copy-done.2), kind=kLoop, calls=%fused_computation.2 | loop fusion | flops 737280 | bytes 1376256 | tf_op jit(solution)/shard_map/sub | solution.py:18
Async XLA Ops:
  0.6 0.7 %copy-start.3 = (s32[1,2,1,1]{1,3,2,0:T(1,128)S(1)}, s32[1,2,1,1]{1,3,2,0:T(1,128)}, u32[]{:S(2)}) copy-start(s32[1,2,1,1]{1,3,2,0:T(1,128)} %param.8) | copy-start | bytes 28
  1.9 40.6 %copy-start = (f32[1,49152]{1,0:T(1,128)S(1)}, f32[1,49152]{1,0:T(1,128)}, u32[]{:S(2)}) copy-start(f32[1,49152]{1,0:T(1,128)} %param.9) | copy-start | bytes 589828
  1.9 40.6 %copy-start.1 = (f32[1,49152]{1,0:T(1,128)S(1)}, f32[1,49152]{1,0:T(1,128)}, u32[]{:S(2)}) copy-start(f32[1,49152]{1,0:T(1,128)} %param.10) | copy-start | bytes 589828
  1.9 40.6 %copy-start.2 = (f32[1,49152]{1,0:T(1,128)S(1)}, f32[1,49152]{1,0:T(1,128)}, u32[]{:S(2)}) copy-start(f32[1,49152]{1,0:T(1,128)} %param.11) | copy-start | bytes 589828

commit v2 on v1

--- a/solution.py
+++ b/solution.py
@@ -17,6 +17,13 @@
     corr_v = new_v / (1.0 - 0.95**10)
     new_w = weight_now - 0.01 * (corr_m / (jnp.sqrt(corr_v) + 1e-08) + 0.1 * weight_now)
     return (new_w, new_m, new_v)
+
+
+def adamw_kernel(grad, weight, moment, second, new_weight, new_moment, new_second):
+    new_w, new_m, new_v = adamw_shard(grad[...], weight[...], moment[...], second[...])
+    new_weight[...] = new_w
+    new_moment[...] = new_m
+    new_second[...] = new_v
 
 
 def dp_digits(mesh):
@@ -37,13 +44,12 @@
     return [(1, 1)] * (3 - len(digits)) + digits
 
 
-def reduce_kernel(digits, micro, acts, cotan, counts, out, acts_out, cotan_out, acts_in, cotan_in, lhs, rhs, grad, got1, got2, got3,
-                  part_send, part_recv, send1, recv1, send2, recv2, send3, recv3):
+def reduce_kernel(digits, micro, pieces, acts, cotan, counts, out, acts_held, cotan_held, acts_out, cotan_out, acts_in, cotan_in, rhs,
+                  grad, got1, got2, got3, load_sem, part_send, part_recv, send1, recv1, send2, recv2, send3, recv3):
     sections = lax.axis_size("section")
     section = lax.axis_index("section")
     dp = lax.axis_index("dp")
     mirror = sections - 1 - section
-    (count_a, stride_a), (count_b, stride_b), (count_c, stride_c) = digits
 
     def moved(step, digit):
         count, stride = digit
@@ -56,50 +62,93 @@
     barrier = pltpu.get_barrier_semaphore()
     for peer in peers:
         pl.semaphore_signal(barrier, inc=1, device_id=peer, device_id_type=MESH)
+    loads = [
+        pltpu.make_async_copy(cotan, cotan_held, load_sem.at[0]),
+        pltpu.make_async_copy(acts.at[1], acts_held.at[1], load_sem.at[1]),
+        pltpu.make_async_copy(acts.at[0], acts_held.at[0], load_sem.at[2]),
+    ]
+    for load in loads:
+        load.start()
 
     rows, depth = acts.shape[1], acts.shape[2]
     width = cotan.shape[2]
     slots = rows // micro
+    shard_rows = out.shape[0]
+    half = shard_rows // 2
+    orders = ((digits[0], digits[1]), (digits[1], digits[0]))
+    last = digits[2]
+    per_row = width // LANES
 
     def masked(k):
-        pieces = []
+        parts = []
         for b in range(micro):
-            block = cotan[k, b * slots:(b + 1) * slots, :].astype(jnp.float32)
+            block = cotan_held[k, b * slots:(b + 1) * slots, :].astype(jnp.float32)
             place = lax.broadcasted_iota(jnp.int32, (slots, width), 0)
-            pieces.append(jnp.where(place < counts[k, b], block, 0.0))
-        return pieces[0] if micro == 1 else jnp.concatenate(pieces, axis=0)
-
-    cotan_out[...] = masked(1)
-    acts_out[...] = acts[1].astype(jnp.float32)
-    pl.semaphore_wait(barrier, len(peers))
+            parts.append(jnp.where(place < counts[b, k], block, 0.0))
+        return parts[0] if micro == 1 else jnp.concatenate(parts, axis=0)
+
+    steps3 = sorted(range(1, last[0]), key=lambda step: -min(step, last[0] - step)) + [0]
+    piece = depth // pieces
+    by_owner = pieces == lax.axis_size("dp")
+    kinds = {"forward": [], "own": [], "mine": []}
+    for step_a in range(digits[0][0]):
+        for step_b in range(digits[1][0]):
+            kind = "forward" if step_a and step_b else "own" if step_a or step_b else "mine"
+            kinds[kind].append((step_a, step_b))
+    groups = [("forward", 0), ("own", 0), ("forward", 1)]
+    groups += [(kind, i) for i in range(len(steps3)) for kind in ("own", "forward", "mine") if (kind, i) not in groups]
+    owners, group_of = [], {}
+    for kind, i in groups:
+        if i < len(steps3):
+            group_of[kind, i] = range(len(owners), len(owners) + len(kinds[kind]))
+            for step_a, step_b in kinds[kind]:
+                owners.append(dp + moved(step_a, digits[0]) + moved(step_b, digits[1]) + moved(steps3[i], last))
+    if not by_owner:
+        owners = list(range(pieces))
+
+    def columns(at):
+        start = owners[at] * piece
+        return pl.ds(start if isinstance(start, int) else pl.multiple_of(start, LANES), piece)
 
     def to_mirror(src, dst, at):
         return pltpu.make_async_remote_copy(
             src_ref=src, dst_ref=dst, send_sem=part_send.at[at], recv_sem=part_recv.at[at],
             device_id=(dp, mirror), device_id_type=MESH)
 
-    exchange = [to_mirror(cotan_out, cotan_in, 0), to_mirror(acts_out, acts_in, 1)]
-    for copy in exchange:
+    exchange = [to_mirror(acts_out.at[at], acts_in.at[at], at) for at in range(pieces)]
+    exchange.append(to_mirror(cotan_out, cotan_in, pieces))
+    loads[0].wait()
+    cotan_out[...] = masked(1)
+    rhs[0:rows, :] = masked(0).astype(jnp.bfloat16)
+    loads[1].wait()
+    for at in range(pieces):
+        acts_out[at] = acts_held[1, :, columns(at)].astype(jnp.float32)
+    pl.semaphore_wait(barrier, len(peers))
+    exchange[pieces].start()
+    for copy in exchange[:pieces]:
         copy.start()
-    lhs[0:rows, :] = acts[0]
-    rhs[0:rows, :] = masked(0).astype(jnp.bfloat16)
-    for copy in exchange:
-        copy.wait_recv()
+    loads[2].wait()
+    exchange[pieces].wait_recv()
     rhs[rows:2 * rows, :] = cotan_in[...].astype(jnp.bfloat16)
-    lhs[rows:2 * rows, :] = acts_in[...].astype(jnp.bfloat16)
-
-    per_row = width // LANES
-    tile = 256
-    for t in range(depth // tile):
-        product = lax.dot_general(
-            lhs[:, t * tile:(t + 1) * tile], rhs[...], (((0,), (0,)), ((), ())), preferred_element_type=jnp.float32)
+
+    def make(at):
+        exchange[at].wait_recv()
+        lhs = jnp.concatenate([acts_held[0, :, columns(at)], acts_in[at].astype(jnp.bfloat16)], axis=0)
+        product = lax.dot_general(lhs, rhs[...], (((0,), (0,)), ((), ())), preferred_element_type=jnp.float32)
+        first = owners[at] * (piece * per_row)
+        if not isinstance(first, int):
+            first = pl.multiple_of(first, 8)
         for c in range(per_row):
-            grad[pl.ds(t * tile * per_row + c, tile, stride=per_row), :] = product[:, c * LANES:(c + 1) * LANES]
-
-    shard_rows = out.shape[0]
-    half = shard_rows // 2
-    orders = ((digits[0], digits[1]), (digits[1], digits[0]))
-    last = digits[2]
+            grad[pl.ds(first + c, piece, stride=per_row), :] = product[:, c * LANES:(c + 1) * LANES]
+
+    def make_group(kind, i):
+        if by_owner and (kind, i) in group_of:
+            for at in group_of.pop((kind, i)):
+                make(at)
+
+    if not by_owner:
+        for at in range(pieces):
+            make(at)
 
     def block(o, step1, step2, step3):
         first, second = orders[o]
@@ -148,8 +197,6 @@
             total += got2[o][(step2 - 1) * last[0] + step3]
         return total
 
-    steps3 = sorted(range(1, last[0]), key=lambda step: -min(step, last[0] - step)) + [0]
-
     def send_forward(i):
         if i < len(steps3):
             for o in range(2):
@@ -174,9 +221,14 @@
             block(o, 0, 0, steps3[i])[...] = arrived2(o, steps3[i])
             start(stage3(o, steps3[i]))
 
+    make_group("forward", 0)
     send_forward(0)
+    make_group("own", 0)
     send_own(0)
+    make_group("forward", 1)
     send_forward(1)
+    for kind, i in list(group_of):
+        make_group(kind, i)
     for i in range(len(steps3)):
         send_second(i)
         send_own(i + 1)
@@ -199,6 +251,8 @@
     width = cotan.shape[3]
     shard_rows = weight.shape[1] // LANES
     half = shard_rows // 2
+    piece = weight.shape[1] // width
+    pieces = depth // piece if piece % LANES == 0 and weight.shape[1] % width == 0 else depth // (2 * LANES)
     counts1 = [(first - 1) * other * digits[2][0] for first, other in ((digits[0][0], digits[1][0]), (digits[1][0], digits[0][0]))]
     counts2 = [(other - 1) * digits[2][0] for other in (digits[1][0], digits[0][0])]
     counts3 = [digits[2][0] - 1] * 2
@@ -209,30 +263,39 @@
     def semaphores(sizes):
         return [pltpu.SemaphoreType.DMA((max(size, 1),)) for size in sizes]
 
+    hbm = pl.BlockSpec(memory_space=pl.ANY)
     vmem = pl.BlockSpec(memory_space=pltpu.VMEM)
     shard = pl.pallas_call(
-        functools.partial(reduce_kernel, digits, micro),
+        functools.partial(reduce_kernel, digits, micro, pieces),
         out_shape=jax.ShapeDtypeStruct((shard_rows, LANES), jnp.float32),
-        in_specs=[vmem, vmem, pl.BlockSpec(memory_space=pltpu.SMEM)],
+        in_specs=[hbm, hbm, pl.BlockSpec(memory_space=pltpu.SMEM)],
         out_specs=vmem,
         scratch_shapes=[
-            pltpu.VMEM((rows, depth), jnp.float32),
+            pltpu.VMEM((2, rows, depth), jnp.bfloat16),
+            pltpu.VMEM((2, rows, width), jnp.bfloat16),
+            pltpu.VMEM((pieces, rows, depth // pieces), jnp.float32),
             pltpu.VMEM((rows, width), jnp.float32),
-            pltpu.VMEM((rows, depth), jnp.float32),
+            pltpu.VMEM((pieces, rows, depth // pieces), jnp.float32),
             pltpu.VMEM((rows, width), jnp.float32),
-            pltpu.VMEM((2 * rows, depth), jnp.bfloat16),
             pltpu.VMEM((2 * rows, width), jnp.bfloat16),
             pltpu.VMEM((depth * width // LANES, LANES), jnp.float32),
             buffers(counts1), buffers(counts2), buffers(counts3),
-            pltpu.SemaphoreType.DMA((2,)), pltpu.SemaphoreType.DMA((2,)),
+            pltpu.SemaphoreType.DMA((3,)), pltpu.SemaphoreType.DMA((pieces + 1,)), pltpu.SemaphoreType.DMA((pieces + 1,)),
             semaphores(counts1), semaphores(counts1), semaphores(counts2), semaphores(counts2),
             semaphores(counts3), semaphores(counts3),
         ],
         compiler_params=pltpu.CompilerParams(collective_id=0, has_side_effects=True),
         name="reduce_grad",
-    )(acts[0], cotan[0], counts[0, :, 0, :])
-    new_w, new_m, new_v = adamw_shard(shard.reshape(1, -1), weight, moment, second)
-    return (new_w, new_m, new_v)
+    )(acts[0], cotan[0], counts[0, :, 0, :].T)
+    flat = jax.ShapeDtypeStruct((shard_rows, LANES), jnp.float32)
+    outs = pl.pallas_call(
+        adamw_kernel,
+        out_shape=(flat, flat, flat),
+        in_specs=[vmem] * 4,
+        out_specs=(vmem, vmem, vmem),
+        name="adamw",
+    )(shard, *(array.reshape(shard_rows, LANES) for array in (weight, moment, second)))
+    return tuple(array.reshape(weight.shape) for array in outs)
 
 
 def solution(mesh):

time: 45.8 us -> 41.3 us (0.902)
  other arithmetic: 3.07 us -> 0 us
  local copies, waits for them, and re-layouts: 1.31 us -> 0 us
    sub x1 -> x0, other arithmetic: 3.07 us -> none  [adamw_shard(): weight_now - 0.01 * (corr_m / (jnp.sqrt(corr_v) + 1e-08) + 0.1 * weight_now)]
    unnamed x8 -> x0, local copies, waits for them, and re-layouts: 0.66 us -> none
    squeeze x1 -> x0, local copies, waits for them, and re-layouts: 0.65 us -> none  [shards(): counts[0, :, 0, :]]
    pallas_call x1 -> x2, Pallas kernels: 40.6 us -> 40.5 us  [the longest x1 38.3 us: shards(): pl.pallas_call(functools.partial(reduce_kernel, digits, micro, pieces), o...]
where the time goes in v2:
time: 41.3 us; the launch traced here: 41.1 us
  Pallas kernels  40.5 us (98%)
  between operations  0.64 us (2%)
    pallas_call x1, Pallas kernels, shards(): pl.pallas_call(functools.partial(reduce_kernel, digits, micro, pieces), o...  38.3 us
    pallas_call x1, Pallas kernels, shards(): pl.pallas_call(adamw_kernel, out_shape=(flat, flat, flat), in_specs=[vmem...  2.15 us

profile of v2, /device:TPU:0, one launch (start us, length us, event | category | flops | bytes accessed | tf_op | source)
XLA Modules:
  0.0 41.1 jit_solution(17597594943153785325)
XLA Ops:
  0.6 38.3 %reduce_grad.1.grad = f32[384,128]{1,0:T(8,128)} custom-call(bf16[2,128,2048]{2,1,0:T(8,128)(2,1)} %bitcast.9, bf16[2,128,384]{2,1,0:T(8,128)(2,1)} %bitcast.13, s32[1,2]{1,0:T(1,128)} %bitcast.14), custom_call_target="tpu_custom_call" | custom-call | tf_op jit(solution)/shard_map/reduce_grad/pallas_call | solution.py:268
  39.0 2.2 %adamw.1 = (f32[384,128]{1,0:T(8,128)}, f32[384,128]{1,0:T(8,128)}, f32[384,128]{1,0:T(8,128)}) custom-call(f32[384,128]{1,0:T(8,128)} %reduce_grad.1.grad, f32[384,128]{1,0:T(8,128)} %bitcast.10, f32[384,128]{1,0:T(8,128)} %bitcast.11, f32[384,128]{1,0:T(8,128)} %bitcast.12), custom_call_target="tpu_custom_call" | custom-call | tf_op jit(solution)/shard_map/adamw/pallas_call | solution.py:291

commit v3 on v2

--- a/solution.py
+++ b/solution.py
@@ -44,8 +44,20 @@
     return [(1, 1)] * (3 - len(digits)) + digits
 
 
+def axis_orders(digits):
+    a, b, c = digits
+    return [(a, b, c), (b, a, c), (c, a, b), (c, b, a)]
+
+
+def row_spans(shard_rows):
+    late = shard_rows // 128 * 8
+    early = (shard_rows - 2 * late) // 2
+    spans = [(0, early), (early, early), (2 * early, late), (2 * early + late, late)]
+    return spans[:4 if late else 2]
+
+
 def reduce_kernel(digits, micro, pieces, acts, cotan, counts, out, acts_held, cotan_held, acts_out, cotan_out, acts_in, cotan_in, rhs,
-                  grad, got1, got2, got3, load_sem, part_send, part_recv, send1, recv1, send2, recv2, send3, recv3):
+                  grad, got1, got2, got3, entered, load_sem, part_send, part_recv, send1, recv1, send2, recv2, send3, recv3):
     sections = lax.axis_size("section")
     section = lax.axis_index("section")
     dp = lax.axis_index("dp")
@@ -56,12 +68,18 @@
         mine = lax.rem(lax.div(dp, stride), count)
         return (lax.rem(mine + step, count) - mine) * stride
 
+    length = digits[2][0]
+    place_c = lax.rem(lax.div(dp, digits[2][1]), length)
+    left, right = (dp - digits[2][1], section), (dp + digits[2][1], section)
+    has_left, has_right = place_c > 0, place_c < length - 1
     peers = [(dp, mirror)]
-    for digit in digits:
+    for digit in digits[:2]:
         peers += [(dp + moved(step, digit), section) for step in range(1, digit[0])]
     barrier = pltpu.get_barrier_semaphore()
     for peer in peers:
         pl.semaphore_signal(barrier, inc=1, device_id=peer, device_id_type=MESH)
+    pl.when(has_left)(lambda: pl.semaphore_signal(barrier, inc=1, device_id=left, device_id_type=MESH))
+    pl.when(has_right)(lambda: pl.semaphore_signal(barrier, inc=1, device_id=right, device_id_type=MESH))
     loads = [
         pltpu.make_async_copy(cotan, cotan_held, load_sem.at[0]),
         pltpu.make_async_copy(acts.at[1], acts_held.at[1], load_sem.at[1]),
@@ -74,8 +92,8 @@
     width = cotan.shape[2]
     slots = rows // micro
     shard_rows = out.shape[0]
-    half = shard_rows // 2
-    orders = ((digits[0], digits[1]), (digits[1], digits[0]))
+    orders = axis_orders(digits)
+    spans = row_spans(shard_rows)
     last = digits[2]
     per_row = width // LANES
 
@@ -123,7 +141,23 @@
     loads[1].wait()
     for at in range(pieces):
         acts_out[at] = acts_held[1, :, columns(at)].astype(jnp.float32)
-    pl.semaphore_wait(barrier, len(peers))
+    pl.semaphore_wait(barrier, len(peers) + has_left.astype(jnp.int32) + has_right.astype(jnp.int32))
+
+    def tell_right():
+        pl.semaphore_signal(entered.at[0], inc=1, device_id=right, device_id_type=MESH)
+
+    def tell_left():
+        pl.semaphore_signal(entered.at[1], inc=1, device_id=left, device_id_type=MESH)
+
+    def hand_on():
+        for k in range(1, length - 1):
+            pl.when(place_c > k)(lambda: pl.semaphore_wait(entered.at[0], 1))
+            pl.when(jnp.logical_and(place_c > k, has_right))(tell_right)
+            pl.when(place_c < length - 1 - k)(lambda: pl.semaphore_wait(entered.at[1], 1))
+            pl.when(jnp.logical_and(place_c < length - 1 - k, has_left))(tell_left)
+
+    pl.when(jnp.logical_and(has_left, has_right))(tell_right)
+    pl.when(jnp.logical_and(has_left, has_right))(tell_left)
     exchange[pieces].start()
     for copy in exchange[:pieces]:
         copy.start()
@@ -151,13 +185,13 @@
             make(at)
 
     def block(o, step1, step2, step3):
-        first, second = orders[o]
-        owner = dp + moved(step1, first) + moved(step2, second) + moved(step3, last)
-        return grad.at[pl.ds(pl.multiple_of(owner * shard_rows + o * half, 8), half), :]
+        first, second, third = orders[o]
+        owner = dp + moved(step1, first) + moved(step2, second) + moved(step3, third)
+        return grad.at[pl.ds(pl.multiple_of(owner * shard_rows + spans[o][0], 8), spans[o][1]), :]
 
     def base1(o, step1, step2, step3):
-        first, second = orders[o]
-        return ((step1 - 1) * second[0] + step2) * last[0] + step3
+        first, second, third = orders[o]
+        return ((step1 - 1) * second[0] + step2) * third[0] + step3
 
     def stage1(o, step1, step2, step3):
         at = base1(o, step1, step2, step3)
@@ -166,7 +200,7 @@
             device_id=(dp + moved(step1, orders[o][0]), section), device_id_type=MESH)
 
     def stage2(o, step2, step3):
-        at = (step2 - 1) * last[0] + step3
+        at = (step2 - 1) * orders[o][2][0] + step3
         return pltpu.make_async_remote_copy(
             src_ref=block(o, 0, step2, step3), dst_ref=got2[o].at[at], send_sem=send2[o].at[at], recv_sem=recv2[o].at[at],
             device_id=(dp + moved(step2, orders[o][1]), section), device_id_type=MESH)
@@ -175,7 +209,7 @@
         at = step3 - 1
         return pltpu.make_async_remote_copy(
             src_ref=block(o, 0, 0, step3), dst_ref=got3[o].at[at], send_sem=send3[o].at[at], recv_sem=recv3[o].at[at],
-            device_id=(dp + moved(step3, last), section), device_id_type=MESH)
+            device_id=(dp + moved(step3, orders[o][2]), section), device_id_type=MESH)
 
     started = []
 
@@ -194,7 +228,7 @@
         total = arrived1(o, 0, step3)
         for step2 in range(1, orders[o][1][0]):
             stage2(o, step2, step3).wait_recv()
-            total += got2[o][(step2 - 1) * last[0] + step3]
+            total += got2[o][(step2 - 1) * orders[o][2][0] + step3]
         return total
 
     def send_forward(i):
@@ -220,6 +254,28 @@
         for o in range(2):
             block(o, 0, 0, steps3[i])[...] = arrived2(o, steps3[i])
             start(stage3(o, steps3[i]))
+
+    late = range(2, len(spans))
+
+    def late_first():
+        for o in late:
+            for step1 in steps3[:-1]:
+                for step2 in reversed(range(orders[o][1][0])):
+                    for step3 in reversed(range(orders[o][2][0])):
+                        start(stage1(o, step1, step2, step3))
+
+    def late_second():
+        for o in late:
+            for step2 in range(1, orders[o][1][0]):
+                for step3 in reversed(range(orders[o][2][0])):
+                    block(o, 0, step2, step3)[...] = arrived1(o, step2, step3)
+                    start(stage2(o, step2, step3))
+
+    def late_third():
+        for o in late:
+            for step3 in range(1, orders[o][2][0]):
+                block(o, 0, 0, step3)[...] = arrived2(o, step3)
+                start(stage3(o, step3))
 
     make_group("forward", 0)
     send_forward(0)
@@ -229,18 +285,28 @@
     send_forward(1)
     for kind, i in list(group_of):
         make_group(kind, i)
+    hand_on()
+    late_first()
     for i in range(len(steps3)):
         send_second(i)
         send_own(i + 1)
         send_forward(i + 2)
         if i >= 1:
             send_third(i - 1)
-    for o in range(2):
+        if i == len(steps3) - 3:
+            late_second()
+        if i == len(steps3) - 2:
+            late_third()
+    if len(steps3) < 3:
+        late_second()
+    if len(steps3) < 2:
+        late_third()
+    for o in reversed(range(len(spans))):
         total = arrived2(o, 0)
-        for step3 in range(1, last[0]):
+        for step3 in range(1, orders[o][2][0]):
             stage3(o, step3).wait_recv()
             total += got3[o][step3 - 1]
-        out[o * half:(o + 1) * half, :] = total
+        out[spans[o][0]:spans[o][0] + spans[o][1], :] = total
     for copy in exchange + started:
         copy.wait_send()
 
@@ -250,15 +316,17 @@
     rows, depth = acts.shape[2], acts.shape[3]
     width = cotan.shape[3]
     shard_rows = weight.shape[1] // LANES
-    half = shard_rows // 2
     piece = weight.shape[1] // width
     pieces = depth // piece if piece % LANES == 0 and weight.shape[1] % width == 0 else depth // (2 * LANES)
-    counts1 = [(first - 1) * other * digits[2][0] for first, other in ((digits[0][0], digits[1][0]), (digits[1][0], digits[0][0]))]
-    counts2 = [(other - 1) * digits[2][0] for other in (digits[1][0], digits[0][0])]
-    counts3 = [digits[2][0] - 1] * 2
+    orders = axis_orders(digits)
+    spans = row_spans(shard_rows)
+    orders = orders[:len(spans)]
+    counts1 = [(first[0] - 1) * second[0] * third[0] for first, second, third in orders]
+    counts2 = [(second[0] - 1) * third[0] for first, second, third in orders]
+    counts3 = [third[0] - 1 for first, second, third in orders]
 
     def buffers(sizes):
-        return [pltpu.VMEM((max(size, 1), half, LANES), jnp.float32) for size in sizes]
+        return [pltpu.VMEM((max(size, 1), span[1], LANES), jnp.float32) for size, span in zip(sizes, spans)]
 
     def semaphores(sizes):
         return [pltpu.SemaphoreType.DMA((max(size, 1),)) for size in sizes]
@@ -280,6 +348,7 @@
             pltpu.VMEM((2 * rows, width), jnp.bfloat16),
             pltpu.VMEM((depth * width // LANES, LANES), jnp.float32),
             buffers(counts1), buffers(counts2), buffers(counts3),
+            pltpu.SemaphoreType.REGULAR((2,)),
             pltpu.SemaphoreType.DMA((3,)), pltpu.SemaphoreType.DMA((pieces + 1,)), pltpu.SemaphoreType.DMA((pieces + 1,)),
             semaphores(counts1), semaphores(counts1), semaphores(counts2), semaphores(counts2),
             semaphores(counts3), semaphores(counts3),

time: 41.3 us -> 40.3 us (0.976)
  Pallas kernels: 40.5 us -> 39.5 us
    pallas_call x1, Pallas kernels: 38.3 us -> 37.4 us  [shards(): pl.pallas_call(functools.partial(reduce_kernel, digits, micro, pieces), o...]
where the time goes in v3:
time: 40.3 us; the launch traced here: 40.2 us
  Pallas kernels  39.5 us (98%)
  between operations  0.64 us (2%)
    pallas_call x1, Pallas kernels, shards(): pl.pallas_call(functools.partial(reduce_kernel, digits, micro, pieces), o...  37.4 us
    pallas_call x1, Pallas kernels, shards(): pl.pallas_call(adamw_kernel, out_shape=(flat, flat, flat), in_specs=[vmem...  2.15 us

profile of v3, /device:TPU:0, one launch (start us, length us, event | category | flops | bytes accessed | tf_op | source)
XLA Modules:
  0.0 40.2 jit_solution(15539970587583118894)
XLA Ops:
  0.6 37.4 %reduce_grad.1.grad = f32[384,128]{1,0:T(8,128)} custom-call(bf16[2,128,2048]{2,1,0:T(8,128)(2,1)} %bitcast.9, bf16[2,128,384]{2,1,0:T(8,128)(2,1)} %bitcast.13, s32[1,2]{1,0:T(1,128)} %bitcast.14), custom_call_target="tpu_custom_call" | custom-call | tf_op jit(solution)/shard_map/reduce_grad/pallas_call | solution.py:336
  38.0 2.2 %adamw.1 = (f32[384,128]{1,0:T(8,128)}, f32[384,128]{1,0:T(8,128)}, f32[384,128]{1,0:T(8,128)}) custom-call(f32[384,128]{1,0:T(8,128)} %reduce_grad.1.grad, f32[384,128]{1,0:T(8,128)} %bitcast.10, f32[384,128]{1,0:T(8,128)} %bitcast.11, f32[384,128]{1,0:T(8,128)} %bitcast.12), custom_call_target="tpu_custom_call" | custom-call | tf_op jit(solution)/shard_map/adamw/pallas_call | solution.py:360

commit v4 on v3

--- a/solution.py
+++ b/solution.py
@@ -57,7 +57,7 @@
 
 
 def reduce_kernel(digits, micro, pieces, acts, cotan, counts, out, acts_held, cotan_held, acts_out, cotan_out, acts_in, cotan_in, rhs,
-                  grad, got1, got2, got3, entered, load_sem, part_send, part_recv, send1, recv1, send2, recv2, send3, recv3):
+                  grad, got1, got2, got3, load_sem, part_send, part_recv, send1, recv1, send2, recv2, send3, recv3):
     sections = lax.axis_size("section")
     section = lax.axis_index("section")
     dp = lax.axis_index("dp")
@@ -68,18 +68,12 @@
         mine = lax.rem(lax.div(dp, stride), count)
         return (lax.rem(mine + step, count) - mine) * stride
 
-    length = digits[2][0]
-    place_c = lax.rem(lax.div(dp, digits[2][1]), length)
-    left, right = (dp - digits[2][1], section), (dp + digits[2][1], section)
-    has_left, has_right = place_c > 0, place_c < length - 1
     peers = [(dp, mirror)]
-    for digit in digits[:2]:
+    for digit in digits:
         peers += [(dp + moved(step, digit), section) for step in range(1, digit[0])]
     barrier = pltpu.get_barrier_semaphore()
     for peer in peers:
         pl.semaphore_signal(barrier, inc=1, device_id=peer, device_id_type=MESH)
-    pl.when(has_left)(lambda: pl.semaphore_signal(barrier, inc=1, device_id=left, device_id_type=MESH))
-    pl.when(has_right)(lambda: pl.semaphore_signal(barrier, inc=1, device_id=right, device_id_type=MESH))
     loads = [
         pltpu.make_async_copy(cotan, cotan_held, load_sem.at[0]),
         pltpu.make_async_copy(acts.at[1], acts_held.at[1], load_sem.at[1]),
@@ -115,11 +109,12 @@
             kinds[kind].append((step_a, step_b))
     groups = [("forward", 0), ("own", 0), ("forward", 1)]
     groups += [(kind, i) for i in range(len(steps3)) for kind in ("own", "forward", "mine") if (kind, i) not in groups]
-    owners, group_of = [], {}
+    owners, places, group_of = [], [], {}
     for kind, i in groups:
         if i < len(steps3):
             group_of[kind, i] = range(len(owners), len(owners) + len(kinds[kind]))
             for step_a, step_b in kinds[kind]:
+                places.append((step_a, step_b, steps3[i]))
                 owners.append(dp + moved(step_a, digits[0]) + moved(step_b, digits[1]) + moved(steps3[i], last))
     if not by_owner:
         owners = list(range(pieces))
@@ -141,23 +136,7 @@
     loads[1].wait()
     for at in range(pieces):
         acts_out[at] = acts_held[1, :, columns(at)].astype(jnp.float32)
-    pl.semaphore_wait(barrier, len(peers) + has_left.astype(jnp.int32) + has_right.astype(jnp.int32))
-
-    def tell_right():
-        pl.semaphore_signal(entered.at[0], inc=1, device_id=right, device_id_type=MESH)
-
-    def tell_left():
-        pl.semaphore_signal(entered.at[1], inc=1, device_id=left, device_id_type=MESH)
-
-    def hand_on():
-        for k in range(1, length - 1):
-            pl.when(place_c > k)(lambda: pl.semaphore_wait(entered.at[0], 1))
-            pl.when(jnp.logical_and(place_c > k, has_right))(tell_right)
-            pl.when(place_c < length - 1 - k)(lambda: pl.semaphore_wait(entered.at[1], 1))
-            pl.when(jnp.logical_and(place_c < length - 1 - k, has_left))(tell_left)
-
-    pl.when(jnp.logical_and(has_left, has_right))(tell_right)
-    pl.when(jnp.logical_and(has_left, has_right))(tell_left)
+    pl.semaphore_wait(barrier, len(peers))
     exchange[pieces].start()
     for copy in exchange[:pieces]:
         copy.start()
@@ -179,10 +158,13 @@
         if by_owner and (kind, i) in group_of:
             for at in group_of.pop((kind, i)):
                 make(at)
-
+                made.append(places[at])
+
+    made = []
     if not by_owner:
         for at in range(pieces):
             make(at)
+        made += places
 
     def block(o, step1, step2, step3):
         first, second, third = orders[o]
@@ -257,12 +239,10 @@
 
     late = range(2, len(spans))
 
-    def late_first():
+    def late_first(step2, step3, step1):
         for o in late:
-            for step1 in steps3[:-1]:
-                for step2 in reversed(range(orders[o][1][0])):
-                    for step3 in reversed(range(orders[o][2][0])):
-                        start(stage1(o, step1, step2, step3))
+            if step1:
+                start(stage1(o, step1, *((step2, step3) if orders[o][1] is digits[0] else (step3, step2))))
 
     def late_second():
         for o in late:
@@ -277,25 +257,37 @@
                 block(o, 0, 0, step3)[...] = arrived2(o, step3)
                 start(stage3(o, step3))
 
+    def send_late():
+        while made:
+            late_first(*made.pop(0))
+
+    end = len(steps3) - 1
     make_group("forward", 0)
     send_forward(0)
     make_group("own", 0)
     send_own(0)
+    send_late()
     make_group("forward", 1)
-    send_forward(1)
+    if end > 1:
+        send_forward(1)
+    send_late()
     for kind, i in list(group_of):
         make_group(kind, i)
-    hand_on()
-    late_first()
-    for i in range(len(steps3)):
+        send_late()
+    for i in range(end + 1):
+        if i == end and i:
+            send_third(i - 1)
         send_second(i)
+        if i == end - 1:
+            send_forward(end)
         send_own(i + 1)
-        send_forward(i + 2)
-        if i >= 1:
+        if i + 2 < end:
+            send_forward(i + 2)
+        if 1 <= i < end:
             send_third(i - 1)
-        if i == len(steps3) - 3:
+        if i == end - 2:
             late_second()
-        if i == len(steps3) - 2:
+        if i == end - 1:
             late_third()
     if len(steps3) < 3:
         late_second()
@@ -348,7 +340,6 @@
             pltpu.VMEM((2 * rows, width), jnp.bfloat16),
             pltpu.VMEM((depth * width // LANES, LANES), jnp.float32),
             buffers(counts1), buffers(counts2), buffers(counts3),
-            pltpu.SemaphoreType.REGULAR((2,)),
             pltpu.SemaphoreType.DMA((3,)), pltpu.SemaphoreType.DMA((pieces + 1,)), pltpu.SemaphoreType.DMA((pieces + 1,)),
             semaphores(counts1), semaphores(counts1), semaphores(counts2), semaphores(counts2),
             semaphores(counts3), semaphores(counts3),

time: 40.3 us -> 38.8 us (0.963)
  Pallas kernels: 39.5 us -> 38 us
    pallas_call x1, Pallas kernels: 37.4 us -> 35.8 us  [shards(): pl.pallas_call(functools.partial(reduce_kernel, digits, micro, pieces), o...]
where the time goes in v4:
time: 38.8 us; the launch traced here: 38.6 us
  Pallas kernels  38 us (98%)
  between operations  0.64 us (2%)
    pallas_call x1, Pallas kernels, shards(): pl.pallas_call(functools.partial(reduce_kernel, digits, micro, pieces), o...  35.8 us
    pallas_call x1, Pallas kernels, shards(): pl.pallas_call(adamw_kernel, out_shape=(flat, flat, flat), in_specs=[vmem...  2.15 us

profile of v4, /device:TPU:0, one launch (start us, length us, event | category | flops | bytes accessed | tf_op | source)
XLA Modules:
  0.0 38.6 jit_solution(3262755187132070482)
XLA Ops:
  0.6 35.8 %reduce_grad.1.grad = f32[384,128]{1,0:T(8,128)} custom-call(bf16[2,128,2048]{2,1,0:T(8,128)(2,1)} %bitcast.9, bf16[2,128,384]{2,1,0:T(8,128)(2,1)} %bitcast.13, s32[1,2]{1,0:T(1,128)} %bitcast.14), custom_call_target="tpu_custom_call" | custom-call | tf_op jit(solution)/shard_map/reduce_grad/pallas_call | solution.py:328
  36.4 2.2 %adamw.1 = (f32[384,128]{1,0:T(8,128)}, f32[384,128]{1,0:T(8,128)}, f32[384,128]{1,0:T(8,128)}) custom-call(f32[384,128]{1,0:T(8,128)} %reduce_grad.1.grad, f32[384,128]{1,0:T(8,128)} %bitcast.10, f32[384,128]{1,0:T(8,128)} %bitcast.11, f32[384,128]{1,0:T(8,128)} %bitcast.12), custom_call_target="tpu_custom_call" | custom-call | tf_op jit(solution)/shard_map/adamw/pallas_call | solution.py:351
